TPU v7x, 256 devices: a whole 4x4x8 slice. The times are simulated.
256 devices in a mesh: tm: 32 (over z, x), rows: 8 (over y, core).
Axes of the slice: x: 4, y: 4, z: 8, core: 2. Of those that a mesh axis runs over, the one named last changes fastest.
Arguments:
- x_start: float32 [1, 16, 128, 128], P(None, None, 'rows'), may hold values from -6 to 6
- noise: float32 [32, 1, 16, 128, 128], P('tm', None, None, 'rows'), may hold values from -6 to 6
- fresh: float32 [5, 1, 16, 128, 128], P(None, None, None, 'rows'), may hold values from -6 to 6
- sched: int32 [38], replicated, may hold values from 888 to 999, as said below
- conv_in: bfloat16 [3, 3, 192, 16], replicated, may hold values from -0.5 to 0.5
- conv_mid: bfloat16 [3, 3, 192, 192], replicated, may hold values from -0.15625 to 0.15625
- conv_out: bfloat16 [3, 3, 16, 192], replicated, may hold values from -0.15625 to 0.15625
- time_weight: bfloat16 [192, 192], replicated, may hold values from -0.4375 to 0.4375
Outputs:
- trajectory: float32 [2, 32, 1, 16, 128, 128], P(None, 'tm', None, None, 'rows')
Inputs may be any that keep to these rules, and one draw needn't show every extreme that they name: sched[0] = 999 and each entry is 1 to 3 below the one before it.
All inputs are finite; a program needn't handle non-finite values.
Results may differ from a plain program's by a relative error of at most 0.00055.
Values may be sent and summed in bfloat16 or wider, within the bound.
No kernel may reach another device: no remote copies, remote signals or barrier semaphores. Data moves between devices by JAX's collectives and lax.ppermute only.
A program may use at most 64 MiB of HBM per device.

v0:
```python
import jax
import jax.numpy as jnp
from jax import lax
from jax.sharding import PartitionSpec as P

STEPS = 1000
SWEEPS = 2
RETIRE = 5
ROUNDS = 2
log_base = 9.210340371976184


def extended(array, sides, width):
    for axis, dim in sides:
        size, length = (lax.axis_size(axis), array.shape[dim])
        up = [(i, (i + 1) % size) for i in range(size - 1)]
        down = [(j, i) for i, j in up]
        last = lax.slice_in_dim(array, length - width, length, axis=dim)
        initial = lax.slice_in_dim(array, 0, width, axis=dim)
        before = lax.ppermute(last, axis, up)
        after = lax.ppermute(initial, axis, down)
        array = jnp.concatenate([before, array, after], axis=dim)
    return array


def entering_2(value, axis, join, neutral):
    count, mine = (lax.axis_size(axis), lax.axis_index(axis))
    pieces = lax.all_gather(value, axis)
    subtotal = jnp.full_like(value, 0) + jnp.asarray(neutral, value.dtype)

    def turn(position, subtotal):
        longer = join(subtotal, pieces[position])
        return jnp.where(position < mine, longer, subtotal)

    return lax.fori_loop(0, count - 1, turn, subtotal)


def from_behind(array, axis, by):
    length = lax.axis_size(axis)
    pairs = [(i, i + by) for i in range(length) if 0 <= i + by < length]
    return lax.ppermute(array, axis, pairs)


def broadcast(value, axis, source):
    kept = jnp.where(lax.axis_index(axis) == source, value, 0).astype(value.dtype)
    return lax.psum(kept, axis)


def plan_table(total_steps):
    positions = jnp.arange(total_steps).astype(jnp.float32)
    betas = 0.0001 + (0.02 - 0.0001) * positions / (total_steps - 1)
    return jnp.cumsum(jnp.log(1.0 - betas))


def lookup(table, position):
    return jnp.sum(jnp.where(jnp.arange(table.shape[0]) == position, table, 0.0))


def coefficients(log_now, log_next):
    retained = jnp.exp(log_now - log_next)
    bar_now = jnp.exp(log_now)
    bar_next = jnp.exp(log_next)
    keep = 1.0 / jnp.sqrt(retained) - 1.0
    predict = -(1.0 - retained) / (jnp.sqrt(1.0 - bar_now) * jnp.sqrt(retained))
    spread = jnp.sqrt((1.0 - bar_next) / (1.0 - bar_now) * (1.0 - retained))
    return (keep, predict, spread)


def time_features(now_value, width):
    half = width // 2
    freqs = jnp.exp(-log_base * jnp.arange(half).astype(jnp.float32) / half)
    angles = now_value * freqs
    return jnp.concatenate([jnp.sin(angles), jnp.cos(angles)], axis=-1)


def convolve(padded, weight, out_rows):
    columns = padded.shape[3]
    widened = jnp.pad(padded, ((0, 0), (0, 0), (0, 0), (1, 1)))
    running = None
    for row_tap in range(3):
        for col_tap in range(3):
            shifted = widened[:, :, row_tap : row_tap + out_rows, col_tap : col_tap + columns]
            product_term = jnp.einsum(
                "oc,fcrw->forw",
                weight[row_tap, col_tap],
                shifted,
                preferred_element_type=jnp.float32,
            )
            running = product_term if running is None else running + product_term
    return running


def hidden_rim(values):
    return extended(values, (("rows", 2),), 1)


def drift_network(state, noise_now, keep, predict, spread, embedding, conv_in, conv_mid, conv_out):
    latent = state[0].astype(jnp.bfloat16)
    strip_rows = latent.shape[2]
    padded = extended(latent, (("rows", 2),), 1)
    first = convolve(padded, conv_in, strip_rows) + embedding[None, :, None, None]
    first = jax.nn.silu(first).astype(jnp.bfloat16)
    second = jax.nn.silu(convolve(hidden_rim(first), conv_mid, strip_rows)).astype(jnp.bfloat16)
    predicted = convolve(hidden_rim(second), conv_out, strip_rows)
    return keep * state + predict * predicted[None] + spread * noise_now


def add_terms(earlier, later):
    return earlier + later


def prefix(change):
    return entering_2(change, "tm", add_terms, jnp.zeros_like(change))


def shards(x_start, noise, fresh, sched, conv_in, conv_mid, conv_out, time_weight):
    slot = lax.axis_index("tm")
    slots = lax.axis_size("tm")
    table = plan_table(STEPS)
    hidden_width = conv_mid.shape[2]
    state = x_start[None]
    noise_now = noise
    base_state = state
    snapshots = []
    for round_index in range(ROUNDS):
        position = slot + RETIRE * round_index
        now_step = lax.dynamic_index_in_dim(sched, position, 0, keepdims=False)
        next_step = lax.dynamic_index_in_dim(sched, position + 1, 0, keepdims=False)
        keep, predict, spread = coefficients(lookup(table, now_step), lookup(table, next_step))
        features = time_features(now_step.astype(jnp.float32), hidden_width)
        embedding = jnp.dot(
            features[None], time_weight.astype(jnp.float32), precision=lax.Precision.HIGHEST
        )[0]
        for sweep_index in range(SWEEPS):
            change = drift_network(
                state, noise_now, keep, predict, spread, embedding, conv_in, conv_mid, conv_out
            )
            state = base_state + prefix(change)
        snapshots.append(state)
        if round_index + 1 < ROUNDS:
            moved_state, moved_noise = from_behind((state, noise_now), "tm", -RETIRE)
            entering = slot >= slots - RETIRE
            pick = jnp.clip(round_index * RETIRE + slot - (slots - RETIRE), 0, fresh.shape[0] - 1)
            incoming = lax.dynamic_index_in_dim(fresh, pick, 0, keepdims=True)
            state = jnp.where(entering, state, moved_state)
            noise_now = jnp.where(entering, incoming, moved_noise)
            base_state = broadcast(state, "tm", 0)
    return jnp.stack(snapshots)


def solution(mesh):
    placed = (
        P(None, None, "rows", None),
        P("tm", None, None, "rows", None),
        P(None, None, None, "rows", None),
        P(),
        P(),
        P(),
        P(),
        P(),
    )
    return jax.shard_map(
        shards,
        mesh=mesh,
        in_specs=placed,
        out_specs=P(None, "tm", None, None, "rows", None),
        check_vma=False,
    )
```

profile of v0, /device:TPU:8, one launch (start us, length us, event | category | flops | bytes accessed | tf_op | source)
XLA Modules:
  0.0 735.1 jit_solution(4137733619743370829)
XLA Ops:
  9.5 3.6 collective-permute-start.1
  17.2 3.2 select_reduce_fusion
  29.3 3.6 collective-permute-start.3
  39.6 3.6 collective-permute-start.4
  43.3 2.5 collective-permute-start.5
  51.6 85.8 %all-gather.9.cloned.1.call-done = f32[32,1,16,16,128]{4,3,2,1,0:T(8,128)} async-done(((f32[1,1,16,16,128]{4,3,2,1,0:T(8,128)}), f32[32,1,16,16,128]{4,3,2,1,0:T(8,128)}) %all-gather.9.cloned.1.call-update) | async-done | bytes 4194320 | tf_op jit(solution)/shard_map/all_gather | solution.py:28
  137.3 30.1 %while.56 = (s32[]{:T(128)}, f32[1,1,16,16,128]{4,3,2,1,0:T(8,128)S(1)}, s32[]{:T(128)}, f32[32,1,1,16,16,128]{5,4,3,2,1,0:T(8,128)}, s32[]{:T(128)}, /*index=5*/s32[]{:T(128)}) while((s32[]{:T(128)}, f32[1,1,16,16,128]{4,3,2,1,0:T(8,128)S(1)}, s32[]{:T(128)}, f32[32,1,1,16,16,128]{5,4,3,2,1,0:T(8,128)}, s32[]{:T(128)}, ...), condition=%wide.region_5.6_spmd.clone, body=%wide.region_4.5_spmd.clone.sunk | while | flops 98308 | bytes 393309 | solution.py:35
  169.5 3.6 collective-permute-start.7
  178.6 3.5 collective-permute-start.8
  190.9 3.5 collective-permute-start.10
  204.3 77.6 %all-gather.11.cloned.1.call-done = f32[32,1,16,16,128]{4,3,2,1,0:T(8,128)} async-done(((f32[1,1,16,16,128]{4,3,2,1,0:T(8,128)}), f32[32,1,16,16,128]{4,3,2,1,0:T(8,128)}) %all-gather.11.cloned.1.call-update) | async-done | bytes 4194320 | tf_op jit(solution)/shard_map/all_gather | solution.py:28
  281.9 30.1 %while.57 = (s32[]{:T(128)}, f32[1,1,16,16,128]{4,3,2,1,0:T(8,128)S(1)}, s32[]{:T(128)}, f32[32,1,1,16,16,128]{5,4,3,2,1,0:T(8,128)}, s32[]{:T(128)}, /*index=5*/s32[]{:T(128)}) while((s32[]{:T(128)}, f32[1,1,16,16,128]{4,3,2,1,0:T(8,128)S(1)}, s32[]{:T(128)}, f32[32,1,1,16,16,128]{5,4,3,2,1,0:T(8,128)}, s32[]{:T(128)}, ...), condition=%wide.region_7.8_spmd.clone, body=%wide.region_6.7_spmd.clone.sunk | while | flops 98308 | bytes 393309 | solution.py:35
  316.5 3.4 collective-permute-done.12
  321.9 3.6 collective-permute-start.14
  331.0 3.5 collective-permute-start.15
  343.2 3.5 collective-permute-start.17
  355.4 82.0 %all-gather.13.cloned.1.call-done = f32[32,1,16,16,128]{4,3,2,1,0:T(8,128)} async-done(((f32[1,1,16,16,128]{4,3,2,1,0:T(8,128)}), f32[32,1,16,16,128]{4,3,2,1,0:T(8,128)}) %all-gather.13.cloned.1.call-update) | async-done | bytes 4194320 | tf_op jit(solution)/shard_map/all_gather | solution.py:28
  437.3 30.1 %while.58 = (s32[]{:T(128)}, f32[1,1,16,16,128]{4,3,2,1,0:T(8,128)S(1)}, s32[]{:T(128)}, f32[32,1,1,16,16,128]{5,4,3,2,1,0:T(8,128)}, s32[]{:T(128)}, /*index=5*/s32[]{:T(128)}) while((s32[]{:T(128)}, f32[1,1,16,16,128]{4,3,2,1,0:T(8,128)S(1)}, s32[]{:T(128)}, f32[32,1,1,16,16,128]{5,4,3,2,1,0:T(8,128)}, s32[]{:T(128)}, ...), condition=%wide.region_12.13_spmd.clone, body=%wide.region_11.12_spmd.clone.sunk | while | flops 98308 | bytes 393309 | solution.py:35
  467.5 112.5 %all-reduce.15.cloned.1.call-done = f32[1,1,16,16,128]{4,2,3,1,0:T(8,128)} async-done(((f32[1,1,16,16,128]{4,2,3,1,0:T(8,128)}), f32[1,1,16,16,128]{4,2,3,1,0:T(8,128)}) %all-reduce.15.cloned.1.call-update) | async-done | bytes 131088 | tf_op jit(solution)/shard_map/psum | solution.py:46
  582.9 3.6 collective-permute-start.21
  592.0 3.5 collective-permute-start.22
  604.2 3.5 collective-permute-start.24
  616.0 81.2 %all-gather.15.cloned.1.call-done = f32[32,1,16,16,128]{4,3,2,1,0:T(8,128)} async-done(((f32[1,1,16,16,128]{4,3,2,1,0:T(8,128)}), f32[32,1,16,16,128]{4,3,2,1,0:T(8,128)}) %all-gather.15.cloned.1.call-update) | async-done | bytes 4194320 | tf_op jit(solution)/shard_map/all_gather | solution.py:28
  697.2 30.2 %while.59 = (s32[]{:T(128)}, f32[1,1,16,16,128]{4,3,2,1,0:T(8,128)S(1)}, s32[]{:T(128)}, f32[32,1,1,16,16,128]{5,4,3,2,1,0:T(8,128)}, s32[]{:T(128)}, /*index=5*/s32[]{:T(128)}) while((s32[]{:T(128)}, f32[1,1,16,16,128]{4,3,2,1,0:T(8,128)S(1)}, s32[]{:T(128)}, f32[32,1,1,16,16,128]{5,4,3,2,1,0:T(8,128)}, s32[]{:T(128)}, ...), condition=%wide.region_14.15_spmd.clone, body=%wide.region_13.14_spmd.clone.sunk | while | flops 98308 | bytes 393309 | solution.py:35
  (355 shorter events, 220.2 us)
Async XLA Ops:
  6.5 130.8 %all-gather.9.cloned.1.call-start = ((), (), s32[]{:S(2)}) async-start(), calls=%async_computation.1 | async-start | bytes 4325376 | tf_op jit(solution)/shard_map/all_gather | solution.py:28
  7.6 15.5 %collective-permute-start = (bf16[1,16,1,128]{3,1,2,0:T(8,128)(2,1)S(1)}, bf16[1,16,1,128]{3,1,2,0:T(8,128)(2,1)S(1)}, u32[]{:S(2)}, u32[]{:S(2)}) collective-permute-start(bf16[1,16,1,128]{3,1,2,0:T(8,128)(2,1)S(1)} %get-tuple-element.493), channel_id=1, source_target_pairs={{0,1},{1,2},{2,3},{3,4},{4,5},{5,6},{6,7},{8,9},{9,10},{10,11},{11... | collective-permute-start | bytes 12296 | tf_op jit(solution)/shard_map/ppermute | solution.py:20
  9.5 13.6 %collective-permute-start.1 = (bf16[1,16,1,128]{3,1,2,0:T(8,128)(2,1)S(1)}, bf16[1,16,1,128]{3,1,2,0:T(8,128)(2,1)S(1)}, u32[]{:S(2)}, u32[]{:S(2)}) collective-permute-start(bf16[1,16,1,128]{3,1,2,0:T(8,128)(2,1)S(1)} %get-tuple-element.494), channel_id=1, source_target_pairs={{1,0},{2,1},{3,2},{4,3},{5,4},{6,5},{7,6},{9,8},{10,9},{11,10},{12... | collective-permute-start | bytes 12296 | tf_op jit(solution)/shard_map/ppermute | solution.py:21
  27.4 6.0 collective-permute-start.2
  29.3 5.4 collective-permute-start.3
  39.6 6.3 collective-permute-start.4
  51.5 230.4 %all-gather.11.cloned.1.call-start = ((), (), s32[]{:S(2)}) async-start(), calls=%async_computation.2 | async-start | bytes 4325376 | tf_op jit(solution)/shard_map/all_gather | solution.py:28
  167.6 6.0 collective-permute-start.6
  169.5 5.0 collective-permute-start.7
  178.6 5.9 collective-permute-start.8
  190.9 6.0 collective-permute-start.10
  202.2 235.1 %all-gather.13.cloned.1.call-start = ((), (), s32[]{:S(2)}) async-start(), calls=%async_computation.3 | async-start | bytes 4325376 | tf_op jit(solution)/shard_map/all_gather | solution.py:28
  202.3 151.1 %collective-permute-start.19 = (f32[1,1,16,16,128]{4,2,3,1,0:T(8,128)S(1)}, f32[1,1,16,16,128]{4,2,3,1,0:T(8,128)S(1)}, u32[]{:S(2)}, u32[]{:S(2)}) collective-permute-start(f32[1,1,16,16,128]{4,2,3,1,0:T(8,128)S(1)} %copy.39), channel_id=1, source_target_pairs={{40,0},{48,8},{56,16},{64,24},{72,32},{80,40},{88,48},{96,56},{104... | collective-permute-start | bytes 393224 | tf_op jit(solution)/shard_map/ppermute | solution.py:41
  312.1 7.8 %collective-permute-start.12 = (f32[1,1,16,16,128]{4,2,3,1,0:T(8,128)S(1)}, f32[1,1,16,16,128]{4,2,3,1,0:T(8,128)S(1)}, u32[]{:S(2)}, u32[]{:S(2)}) collective-permute-start(f32[1,1,16,16,128]{4,2,3,1,0:T(8,128)S(1)} %bitcast_add_fusion.4), channel_id=1, source_target_pairs={{40,0},{48,8},{56,16},{64,24},{72,32},{80,40},{88,48},{96,56},{104... | collective-permute-start | bytes 393224 | tf_op jit(solution)/shard_map/ppermute | solution.py:41
  319.9 6.0 collective-permute-start.13
  321.9 5.0 collective-permute-start.14
  331.0 5.9 collective-permute-start.15
  343.2 6.0 collective-permute-start.17
  354.6 225.4 %all-reduce.15.cloned.1.call-start = ((), (), s32[]{:S(2)}) async-start(), calls=%async_computation | async-start | bytes 262144 | tf_op jit(solution)/shard_map/psum | solution.py:46
  355.3 341.9 %all-gather.15.cloned.1.call-start = ((), (), s32[]{:S(2)}) async-start(), calls=%async_computation.4 | async-start | bytes 4325376 | tf_op jit(solution)/shard_map/all_gather | solution.py:28
  580.9 6.0 collective-permute-start.20
  582.9 5.0 collective-permute-start.21
  592.0 5.9 collective-permute-start.22
  604.2 6.1 collective-permute-start.24
  (16 other events, 411.8 us)
Sparse Core Ops, SparseCore 0:
  51.6 85.6 all-gather.8
  202.4 79.5 all-gather.10
  354.7 82.6 all-gather.12
  440.6 139.2 all-reduce.14
  616.2 81.0 all-gather.14
where the time goes:
time: 745 us; the launch traced here: 735 us
  waiting for transfers between devices  455 us (61%)
  other arithmetic  131 us (18%)
  starting transfers between devices  70.8 us (10%)
  matrix products  46.1 us (6%)
  between operations  21.3 us (3%)
  local copies, waits for them, and re-layouts  7.46 us (1%)
    all_gather x4, waiting for transfers between devices, entering_2(): pieces = lax.all_gather(value, axis)  327 us
    select_n x124, other arithmetic, turn(): return jnp.where(position < mine, longer, subtotal)  118 us
    psum x1, waiting for transfers between devices, broadcast(): return lax.psum(kept, axis)  112 us
    dot_general x108, matrix products, convolve(): jnp.einsum('oc,fcrw->forw', weight[row_tap, col_tap], shifted, preferred_...  45.8 us
    ppermute x12, starting transfers between devices, extended(): before = lax.ppermute(last, axis, up)  34.2 us
    ppermute x12, starting transfers between devices, extended(): after = lax.ppermute(initial, axis, down)  33.8 us
  transfers between devices with their start and end apart: 31, of which 17 were waited for; matrix products, arithmetic and copies ran while one was open for 11% of the time, Pallas kernels for 0%

commit v1 on v0

--- a/solution.py
+++ b/solution.py
@@ -43,7 +43,11 @@
 
 def broadcast(value, axis, source):
     kept = jnp.where(lax.axis_index(axis) == source, value, 0).astype(value.dtype)
-    return lax.psum(kept, axis)
+
+    def part_ratios(view):
+        return lax.all_gather(view, axis).sum(axis=0)
+
+    return part_ratios(kept)
 
 
 def plan_table(total_steps):

time: 745 us -> 683 us (0.917)
  waiting for transfers between devices: 455 us -> 389 us
    psum x1 -> x0, waiting for transfers between devices: 112 us -> none  [broadcast(): return lax.psum(kept, axis)]
    all_gather x0 -> x1, waiting for transfers between devices: none -> 52.6 us  [part_ratios(): return lax.all_gather(view, axis).sum(axis=0)]
  transfers between devices with their start and end apart: 31 -> 31, of which waited for: 17 -> 17; matrix products, arithmetic and copies ran while one was open for 11% -> 9% of each run, Pallas kernels for 0% -> 0%
where the time goes in v1:
time: 683 us; the launch traced here: 673 us
  waiting for transfers between devices  389 us (57%)
  other arithmetic  132 us (19%)
  starting transfers between devices  70.8 us (10%)
  matrix products  48 us (7%)
  between operations  21.5 us (3%)
  local copies, waits for them, and re-layouts  8.33 us (1%)
    all_gather x4, waiting for transfers between devices, entering_2(): pieces = lax.all_gather(value, axis)  321 us
    select_n x124, other arithmetic, turn(): return jnp.where(position < mine, longer, subtotal)  118 us
    all_gather x1, waiting for transfers between devices, part_ratios(): return lax.all_gather(view, axis).sum(axis=0)  52.6 us
    dot_general x108, matrix products, convolve(): jnp.einsum('oc,fcrw->forw', weight[row_tap, col_tap], shifted, preferred_...  47.8 us
    ppermute x12, starting transfers between devices, extended(): before = lax.ppermute(last, axis, up)  34.4 us
    ppermute x12, starting transfers between devices, extended(): after = lax.ppermute(initial, axis, down)  33.6 us
  transfers between devices with their start and end apart: 31, of which 17 were waited for; matrix products, arithmetic and copies ran while one was open for 9% of the time, Pallas kernels for 0%

profile of v1, /device:TPU:8, one launch (start us, length us, event | category | flops | bytes accessed | tf_op | source)
XLA Modules:
  0.0 673.1 jit_solution(2020015299540152187)
XLA Ops:
  9.5 3.6 collective-permute-start.1
  17.2 3.2 select_reduce_fusion
  29.4 3.6 collective-permute-start.3
  39.8 3.6 collective-permute-start.4
  43.4 2.5 collective-permute-start.5
  51.7 85.8 %all-gather.11.cloned.1.call-done = f32[32,1,16,16,128]{4,3,2,1,0:T(8,128)} async-done(((f32[1,1,16,16,128]{4,3,2,1,0:T(8,128)}), f32[32,1,16,16,128]{4,3,2,1,0:T(8,128)}) %all-gather.11.cloned.1.call-update) | async-done | bytes 4194320 | tf_op jit(solution)/shard_map/all_gather | solution.py:28
  137.5 30.1 %while.56 = (s32[]{:T(128)}, f32[1,1,16,16,128]{4,3,2,1,0:T(8,128)S(1)}, s32[]{:T(128)}, f32[32,1,1,16,16,128]{5,4,3,2,1,0:T(8,128)}, s32[]{:T(128)}, /*index=5*/s32[]{:T(128)}) while((s32[]{:T(128)}, f32[1,1,16,16,128]{4,3,2,1,0:T(8,128)S(1)}, s32[]{:T(128)}, f32[32,1,1,16,16,128]{5,4,3,2,1,0:T(8,128)}, s32[]{:T(128)}, ...), condition=%wide.region_5.6_spmd.clone, body=%wide.region_4.5_spmd.clone.sunk | while | flops 98308 | bytes 393309 | solution.py:35
  169.6 3.6 collective-permute-start.7
  178.8 3.5 collective-permute-start.8
  191.0 3.5 collective-permute-start.10
  205.2 76.9 %all-gather.13.cloned.1.call-done = f32[32,1,16,16,128]{4,3,2,1,0:T(8,128)} async-done(((f32[1,1,16,16,128]{4,3,2,1,0:T(8,128)}), f32[32,1,16,16,128]{4,3,2,1,0:T(8,128)}) %all-gather.13.cloned.1.call-update) | async-done | bytes 4194320 | tf_op jit(solution)/shard_map/all_gather | solution.py:28
  282.0 30.1 %while.57 = (s32[]{:T(128)}, f32[1,1,16,16,128]{4,3,2,1,0:T(8,128)S(1)}, s32[]{:T(128)}, f32[32,1,1,16,16,128]{5,4,3,2,1,0:T(8,128)}, s32[]{:T(128)}, /*index=5*/s32[]{:T(128)}) while((s32[]{:T(128)}, f32[1,1,16,16,128]{4,3,2,1,0:T(8,128)S(1)}, s32[]{:T(128)}, f32[32,1,1,16,16,128]{5,4,3,2,1,0:T(8,128)}, s32[]{:T(128)}, ...), condition=%wide.region_7.8_spmd.clone, body=%wide.region_6.7_spmd.clone.sunk | while | flops 98308 | bytes 393309 | solution.py:35
  316.5 3.5 collective-permute-done.12
  322.0 3.6 collective-permute-start.14
  331.2 3.5 collective-permute-start.15
  343.5 3.7 collective-permute-start.17
  356.0 52.6 %all-gather.15.cloned.1.call-done = f32[32,1,16,16,128]{4,3,2,1,0:T(8,128)} async-done(((f32[1,1,16,16,128]{4,3,2,1,0:T(8,128)}), f32[32,1,16,16,128]{4,3,2,1,0:T(8,128)}) %all-gather.15.cloned.1.call-update) | async-done | bytes 4194320 | tf_op jit(solution)/shard_map/all_gather | solution.py:48
  411.0 78.6 %all-gather.17.cloned.1.call-done = f32[32,1,16,16,128]{4,3,2,1,0:T(8,128)} async-done(((f32[1,1,16,16,128]{4,3,2,1,0:T(8,128)}), f32[32,1,16,16,128]{4,3,2,1,0:T(8,128)}) %all-gather.17.cloned.1.call-update) | async-done | bytes 4194320 | tf_op jit(solution)/shard_map/all_gather | solution.py:28
  489.6 30.1 %while.58 = (s32[]{:T(128)}, f32[1,1,16,16,128]{4,3,2,1,0:T(8,128)S(1)}, s32[]{:T(128)}, f32[32,1,1,16,16,128]{5,4,3,2,1,0:T(8,128)}, s32[]{:T(128)}, /*index=5*/s32[]{:T(128)}) while((s32[]{:T(128)}, f32[1,1,16,16,128]{4,3,2,1,0:T(8,128)S(1)}, s32[]{:T(128)}, f32[32,1,1,16,16,128]{5,4,3,2,1,0:T(8,128)}, s32[]{:T(128)}, ...), condition=%wide.region_12.13_spmd.clone, body=%wide.region_11.12_spmd.clone.sunk | while | flops 98308 | bytes 393309 | solution.py:35
  521.8 3.6 collective-permute-start.21
  530.9 3.5 collective-permute-start.22
  543.1 3.5 collective-permute-start.24
  555.4 79.7 %all-gather.19.cloned.1.call-done = f32[32,1,16,16,128]{4,3,2,1,0:T(8,128)} async-done(((f32[1,1,16,16,128]{4,3,2,1,0:T(8,128)}), f32[32,1,16,16,128]{4,3,2,1,0:T(8,128)}) %all-gather.19.cloned.1.call-update) | async-done | bytes 4194320 | tf_op jit(solution)/shard_map/all_gather | solution.py:28
  635.0 30.2 %while.59 = (s32[]{:T(128)}, f32[1,1,16,16,128]{4,3,2,1,0:T(8,128)S(1)}, s32[]{:T(128)}, f32[32,1,1,16,16,128]{5,4,3,2,1,0:T(8,128)}, s32[]{:T(128)}, /*index=5*/s32[]{:T(128)}) while((s32[]{:T(128)}, f32[1,1,16,16,128]{4,3,2,1,0:T(8,128)S(1)}, s32[]{:T(128)}, f32[32,1,1,16,16,128]{5,4,3,2,1,0:T(8,128)}, s32[]{:T(128)}, ...), condition=%wide.region_14.15_spmd.clone, body=%wide.region_13.14_spmd.clone.sunk | while | flops 98308 | bytes 393309 | solution.py:35
  (357 shorter events, 223.2 us)
Async XLA Ops:
  6.5 130.9 %all-gather.11.cloned.1.call-start = ((), (), s32[]{:S(2)}) async-start(), calls=%async_computation | async-start | bytes 4325376 | tf_op jit(solution)/shard_map/all_gather | solution.py:28
  7.6 15.6 %collective-permute-start = (bf16[1,16,1,128]{3,1,2,0:T(8,128)(2,1)S(1)}, bf16[1,16,1,128]{3,1,2,0:T(8,128)(2,1)S(1)}, u32[]{:S(2)}, u32[]{:S(2)}) collective-permute-start(bf16[1,16,1,128]{3,1,2,0:T(8,128)(2,1)S(1)} %get-tuple-element.509), channel_id=1, source_target_pairs={{0,1},{1,2},{2,3},{3,4},{4,5},{5,6},{6,7},{8,9},{9,10},{10,11},{11... | collective-permute-start | bytes 12296 | tf_op jit(solution)/shard_map/ppermute | solution.py:20
  9.5 13.7 %collective-permute-start.1 = (bf16[1,16,1,128]{3,1,2,0:T(8,128)(2,1)S(1)}, bf16[1,16,1,128]{3,1,2,0:T(8,128)(2,1)S(1)}, u32[]{:S(2)}, u32[]{:S(2)}) collective-permute-start(bf16[1,16,1,128]{3,1,2,0:T(8,128)(2,1)S(1)} %get-tuple-element.510), channel_id=1, source_target_pairs={{1,0},{2,1},{3,2},{4,3},{5,4},{6,5},{7,6},{9,8},{10,9},{11,10},{12... | collective-permute-start | bytes 12296 | tf_op jit(solution)/shard_map/ppermute | solution.py:21
  27.5 6.0 collective-permute-start.2
  29.4 5.4 collective-permute-start.3
  39.8 6.4 collective-permute-start.4
  51.6 230.4 %all-gather.13.cloned.1.call-start = ((), (), s32[]{:S(2)}) async-start(), calls=%async_computation.1 | async-start | bytes 4325376 | tf_op jit(solution)/shard_map/all_gather | solution.py:28
  167.7 6.0 collective-permute-start.6
  169.6 5.0 collective-permute-start.7
  178.8 5.9 collective-permute-start.8
  191.0 6.0 collective-permute-start.10
  202.4 206.2 %all-gather.15.cloned.1.call-start = ((), (), s32[]{:S(2)}) async-start(), calls=%async_computation.2 | async-start | bytes 4325376 | tf_op jit(solution)/shard_map/all_gather | solution.py:48
  203.1 150.8 %collective-permute-start.19 = (f32[1,1,16,16,128]{4,2,3,1,0:T(8,128)}, f32[1,1,16,16,128]{4,2,3,1,0:T(8,128)}, u32[]{:S(2)}, u32[]{:S(2)}) collective-permute-start(f32[1,1,16,16,128]{4,2,3,1,0:T(8,128)} %copy.58), channel_id=1, source_target_pairs={{40,0},{48,8},{56,16},{64,24},{72,32},{80,40},{88,48},{96,56},{104... | collective-permute-start | bytes 393224 | tf_op jit(solution)/shard_map/ppermute | solution.py:41
  312.3 7.8 %collective-permute-start.12 = (f32[1,1,16,16,128]{4,2,3,1,0:T(8,128)S(1)}, f32[1,1,16,16,128]{4,2,3,1,0:T(8,128)S(1)}, u32[]{:S(2)}, u32[]{:S(2)}) collective-permute-start(f32[1,1,16,16,128]{4,2,3,1,0:T(8,128)S(1)} %bitcast_add_fusion.6), channel_id=1, source_target_pairs={{40,0},{48,8},{56,16},{64,24},{72,32},{80,40},{88,48},{96,56},{104... | collective-permute-start | bytes 393224 | tf_op jit(solution)/shard_map/ppermute | solution.py:41
  320.1 6.8 %collective-permute-start.13 = (bf16[1,16,1,128]{3,1,2,0:T(8,128)(2,1)S(1)}, bf16[1,16,1,128]{3,1,2,0:T(8,128)(2,1)S(1)}, u32[]{:S(2)}, u32[]{:S(2)}) collective-permute-start(bf16[1,16,1,128]{3,1,2,0:T(8,128)(2,1)S(1)} %get-tuple-element.505), channel_id=1, source_target_pairs={{0,1},{1,2},{2,3},{3,4},{4,5},{5,6},{6,7},{8,9},{9,10},{10,11},{11... | collective-permute-start | bytes 12296 | tf_op jit(solution)/shard_map/ppermute | solution.py:20
  322.0 5.0 collective-permute-start.14
  326.8 162.8 %all-gather.17.cloned.1.call-start = ((), (), s32[]{:S(2)}) async-start(), calls=%async_computation.3 | async-start | bytes 4325376 | tf_op jit(solution)/shard_map/all_gather | solution.py:28
  331.2 5.9 collective-permute-start.15
  343.5 6.0 collective-permute-start.17
  355.9 279.1 %all-gather.19.cloned.1.call-start = ((), (), s32[]{:S(2)}) async-start(), calls=%async_computation.4 | async-start | bytes 4325376 | tf_op jit(solution)/shard_map/all_gather | solution.py:28
  519.8 6.0 collective-permute-start.20
  521.8 5.0 collective-permute-start.21
  530.9 5.9 collective-permute-start.22
  543.1 6.1 collective-permute-start.24
  (16 other events, 523.1 us)
Sparse Core Ops, SparseCore 0:
  51.8 85.6 all-gather.10
  202.5 79.5 all-gather.12
  326.9 81.6 all-gather.14
  411.0 78.5 all-gather.16
  555.5 79.5 all-gather.18
